TPU v7x, 32 devices: a whole 2x2x4 slice. The times are simulated.
32 devices in a mesh: case: 2 (over y), panel: 4 (over z), slab: 2 (over x), obs: 2 (over core).
Axes of the slice: x: 2, y: 2, z: 4, core: 2. Of those that a mesh axis runs over, the one named last changes fastest.
Arguments:
- loading: bfloat16 [65536, 512], P(('case', 'panel'), 'slab'), parts along dimension 0, may hold values from -6 to 6
- green: bfloat16 [128, 32768], P(('case', 'obs'), 'panel'), parts along dimension 0, may hold values from -0.03125 to 0.03125
- delays: int32 [128, 2048], P(('case', 'obs'), 'panel'), parts along dimension 0, may hold values from 0 to 120
- offsets: int32 [128, 2048], P(('case', 'obs'), 'panel'), parts along dimension 0, may hold values from 0 to 7
- live_groups: int32 [8], P('case'), parts along dimension 0, may hold values from 1 to 4, as said below
Outputs:
- signal: float32 [128, 512], P(('case', 'obs'), 'slab'), parts along dimension 0
There are 2 independent parts, one for each index of `case`. A program takes and returns all parts, laid end to end along the dimension named above; each array names one. Nothing has to cross between parts.
Inputs may be any that keep to these rules, and one draw needn't show every extreme that they name: `live_groups`: in every draw some sector has all 4 groups live while the sector 4/2 positions away has one.
All inputs are finite; a program needn't handle non-finite values.
Results may differ from a plain program's by a relative error of at most 0.0034.
Values may be sent and summed in bfloat16 or wider, within the bound.
A program may use at most 64 MiB of HBM per device.

v0:
```python
import jax
import jax.numpy as jnp
from jax import lax
from jax.sharding import PartitionSpec as P

BP = 16
GB = 128
LAGS = 128


def passed_along(block, axis, distance):
    devices = range(lax.axis_size(axis))
    route = [(i - distance, i) for i in devices if i - distance in devices]
    return lax.ppermute(block, axis, route)


def lagrange_weights(offset_part):
    position = 3.0 + offset_part.astype(jnp.float32) / 8.0
    weights = []
    for tap in range(8):
        factor = jnp.ones_like(position)
        for other in range(8):
            if other != tap:
                factor = factor * (position - other) / (tap - other)
        weights.append(factor)
    return weights


def build_table(delay_part, offset_part, lag_count):
    lag_index = jnp.arange(lag_count, dtype=jnp.int32)[None, :, None]
    relative = lag_index - delay_part[:, None, :]
    weights = lagrange_weights(offset_part)
    table_sum = jnp.zeros(relative.shape, jnp.float32)
    for tap in range(8):
        table_sum = table_sum + jnp.where(relative == tap, weights[tap][:, None, :], 0.0)
    return table_sum.astype(jnp.bfloat16)


def skew_sum(lagged):
    observers, lag_count, samples = lagged.shape
    row_width = samples + lag_count + 1
    padded = jnp.pad(lagged, ((0, 0), (0, 0), (0, lag_count + 1)))
    flattened = padded.reshape(observers, lag_count * row_width)[:, : lag_count * (row_width - 1)]
    return flattened.reshape(observers, lag_count, row_width - 1).sum(axis=1)


def group_signal(load_part, green_part, delay_part, offset_part):
    samples = load_part.shape[1]
    observers = green_part.shape[0]
    blocked_load = load_part.reshape(GB, BP, samples)
    blocked_green = green_part.reshape(observers, GB, BP)
    block_signal = jnp.einsum(
        "obp,bpt->bot", blocked_green, blocked_load, preferred_element_type=jnp.float32
    ).astype(jnp.bfloat16)
    lag_table = build_table(delay_part, offset_part, LAGS)
    lagged = jnp.einsum("olb,bot->olt", lag_table, block_signal, preferred_element_type=jnp.float32)
    return skew_sum(lagged)


def shards(loading, green, delays, offsets, live_groups):
    samples = loading.shape[1]
    observers = green.shape[0]
    group_panels = GB * BP
    own_index = lax.axis_index("panel")
    own_count = live_groups[own_index]

    def slice_group(group):
        start = group * group_panels
        return (
            lax.dynamic_slice_in_dim(loading, start, group_panels, 0),
            lax.dynamic_slice_in_dim(green, start, group_panels, 1),
            lax.dynamic_slice_in_dim(delays, group * GB, GB, 1),
            lax.dynamic_slice_in_dim(offsets, group * GB, GB, 1),
        )

    def add_group(group, summed):
        pieces = slice_group(group)
        return summed + group_signal(pieces[0], pieces[1], pieces[2], pieces[3])

    start_sum = jnp.zeros((observers, samples + LAGS), jnp.float32)
    summed = lax.fori_loop(0, own_count, add_group, start_sum)
    carried = passed_along(summed[:, samples:], "slab", 1)
    local_part = summed[:, :samples] + jnp.pad(carried, ((0, 0), (0, samples - LAGS)))
    signal = lax.psum(local_part, "panel")
    return signal


def solution(mesh):
    placed = (
        P(("case", "panel"), "slab"),
        P(("case", "obs"), "panel"),
        P(("case", "obs"), "panel"),
        P(("case", "obs"), "panel"),
        P("case"),
    )
    return jax.shard_map(
        shards, mesh=mesh, in_specs=placed, out_specs=P(("case", "obs"), "slab"), check_vma=False
    )
```

profile of v0, /device:TPU:6, one launch (start us, length us, event | category | flops | bytes accessed | tf_op | source)
XLA Modules:
  0.0 133.7 jit_solution(11575538647123839793)
XLA Ops:
  0.0 1.3 dynamic_slice.39
  1.3 27.2 %while.14 = (s32[]{:T(128)}, f32[32,384]{1,0:T(8,128)S(1)}, s32[]{:T(128)}, s32[32,512]{1,0:T(8,128)}, s32[32,512]{1,0:T(8,128)}, /*index=5*/bf16[32,8192]{1,0:T...) while((s32[]{:T(128)}, f32[32,384]{1,0:T(8,128)S(1)}, ...), condition=%wide.region_2.3_spmd, body=%wide.region_0.2_spmd.sunk | while | flops 317104128 | bytes 73580824 | solution.py:81
  2.0 0.7 constant_dynamic-slice_fusion.8
  2.8 0.8 multiply_multiply_fusion.9
  3.5 0.9 constant_dynamic-slice_fusion.6
  4.5 0.3 copy.16
  4.8 1.3 constant_dynamic-slice_fusion.7
  6.1 0.8 fusion.45
  6.8 3.5 %fusion.46 = f32[32,128,256]{2,1,0:T(8,128)S(1)} fusion(bf16[128,32,256]{2,1,0:T(8,128)(2,1)S(1)} %fusion.45, f32[32,128]{1,0:T(8,128)S(1)} %get-tuple-element.246, f32[32,128]{1,0:T(8,128)S(1)} %get-tuple-element.247, f32[32,128]{1,0:T(8,128)S(1)} %get-tuple-element.248, f32[32,128]{1,0:T(8,128)S(1)} %get-tuple-element.249, ...), kind=kOutput, calls=%fused_computation.2.clone.1 | convolution fusion | flops 281542656 | bytes 6438912 | tf_op jit(solution)/shard_map/while/body/olb,bot->olt/dot_general | solution.py:56
  10.3 4.4 %pad.17 = f32[32,128,385]{2,1,0:T(8,128)} pad(f32[32,128,256]{2,1,0:T(8,128)S(1)} %fusion.46, f32[]{:T(128)} %constant.358.clone.1..sunk), padding=0_0x0_0x0_129 | pad | bytes 10502148 | tf_op jit(solution)/shard_map/while/body/jit(_pad)/pad | solution.py:42
  14.8 8.4 %reshape.46 = f32[32,49280]{1,0:T(8,128)} reshape(f32[32,128,385]{2,1,0:T(8,128)} %pad.17) | data formatting | bytes 12615680 | tf_op jit(solution)/shard_map/while/body/reshape | solution.py:43
  23.1 0.0 slice-start
  23.1 2.8 %slice-done = f32[32,49152]{1,0:T(8,128)S(1)} async-done(((f32[32,49280]{1,0:T(8,128)}), f32[32,49152]{1,0:T(8,128)S(1)}, s32[]{:S(2)}) %slice-start) | async-done | bytes 6291480 | tf_op jit(solution)/shard_map/while/body/slice | solution.py:43
  25.9 1.1 copy.17
  27.0 0.8 bitcast_reduce_fusion.2
  28.6 1.3 collective-permute-start
  29.9 4.3 %collective-permute-done = f32[32,128]{1,0:T(8,128)S(1)} collective-permute-done((f32[32,128]{1,0:T(8,128)S(1)}, f32[32,128]{1,0:T(8,128)S(1)}, u32[]{:S(2)}, u32[]{:S(2)}) %collective-permute-start) | collective-permute-done | bytes 16416 | tf_op jit(solution)/shard_map/ppermute | solution.py:14
  34.2 99.5 %psum.7 = f32[32,256]{1,0:T(8,128)} all-reduce(f32[32,256]{1,0:T(8,128)S(1)} %pad_add_fusion), channel_id=1, replica_groups=mesh['case'=2,'panel'=4,'slab'=2,'obs'=2] {'panel'}, use_global_device_ids=true, to_apply=%region_3.4 | all-reduce | flops 8192 | bytes 65536 | tf_op jit(solution)/shard_map/psum | solution.py:84
  (4 shorter events, 0.0 us)
Async XLA Ops:
  23.1 2.8 %slice-start = ((f32[32,49280]{1,0:T(8,128)}), f32[32,49152]{1,0:T(8,128)S(1)}, s32[]{:S(2)}) async-start(f32[32,49280]{1,0:T(8,128)} %reshape.46), calls=%async_computation | async-start | bytes 12582912 | tf_op jit(solution)/shard_map/while/body/slice | solution.py:43
  28.6 5.6 %collective-permute-start = (f32[32,128]{1,0:T(8,128)S(1)}, f32[32,128]{1,0:T(8,128)S(1)}, u32[]{:S(2)}, u32[]{:S(2)}) collective-permute-start(f32[32,128]{1,0:T(8,128)S(1)} %slice.16), channel_id=1, source_target_pairs={{0,2},{1,3},{4,6},{5,7},{8,10},{9,11},{12,14},{13,15},{16,18},{17,... | collective-permute-start | bytes 49160 | tf_op jit(solution)/shard_map/ppermute | solution.py:14
where the time goes:
time: 134 us
  blocking collectives  99.5 us (74%)
  local copies, waits for them, and re-layouts  21.2 us (16%)
  waiting for transfers between devices  4.33 us (3%)
  matrix products  4.27 us (3%)
  other arithmetic  1.62 us (1%)
  loops' own time  1.45 us (1%)
    psum x1, blocking collectives, shards(): signal = lax.psum(local_part, 'panel')  99.5 us
    reshape x1, local copies, waits for them, and re-layouts, skew_sum(): padded.reshape(observers, lag_count * row_width)  8.36 us
    pad x1, local copies, waits for them, and re-layouts, skew_sum(): padded = jnp.pad(lagged, ((0, 0), (0, 0), (0, lag_count + 1)))  4.42 us
    ppermute x1, waiting for transfers between devices, passed_along(): return lax.ppermute(block, axis, route)  4.33 us
    dot_general x1, matrix products, group_signal(): jnp.einsum('olb,bot->olt', lag_table, block_signal, preferred_element_typ...  3.5 us
    slice x2, local copies, waits for them, and re-layouts, skew_sum(): padded.reshape(observers, lag_count * row_width)  2.78 us
  transfers between devices with their start and end apart: 1, of which 1 were waited for; matrix products, arithmetic and copies ran while one was open for 0% of the time, Pallas kernels for 0%

commit v1 on v0

v1 whole, which is shorter than its diff:
```python
import functools
import math

import jax
import jax.numpy as jnp
from jax import lax
from jax.experimental import pallas as pl
from jax.experimental.pallas import tpu as pltpu
from jax.sharding import PartitionSpec as P

BP = 16
GB = 128
LAGS = 128
TAPS = 8
KT = 256
LANES = 128
ROWS = 8
LOAD_CHUNKS = 8
UNROLL = 2
MESH = pl.DeviceIdType.MESH


def kernel(panels, slabs, live_ref, load_hbm, green_hbm, delay_hbm, offset_hbm, out_ref,
           load_ref, green_in, green_f32, delay_ref, offset_ref, weight_ref, block_ref, part_ref,
           main_in, tail_in, load_sem, small_sem, main_send, main_recv, tail_send, tail_recv):
    panel = lax.axis_index("panel")
    slab = lax.axis_index("slab")
    n_panels, samples = load_hbm.shape
    observers = green_hbm.shape[0]
    blocks = delay_hbm.shape[1]
    chunks = observers // ROWS
    tiles = n_panels // KT
    per_load = n_panels // LOAD_CHUNKS
    has_next = slab < slabs - 1
    has_prev = slab > 0

    smalls = [pltpu.make_async_copy(src, dst, small_sem.at[i]) for i, (src, dst) in enumerate(
        ((green_hbm, green_in), (delay_hbm, delay_ref), (offset_hbm, offset_ref)))]
    for copy in smalls:
        copy.start()
    loads = []
    for c in range(LOAD_CHUNKS):
        rows = pl.ds(c * per_load, per_load)
        loads.append(pltpu.make_async_copy(load_hbm.at[rows, :], load_ref.at[rows, :], load_sem.at[c]))
        loads[-1].start()

    barrier = pltpu.get_barrier_semaphore()
    for d in range(1, panels):
        pl.semaphore_signal(barrier, inc=1, device_id={"panel": lax.rem(panel + d, panels)}, device_id_type=MESH)

    @pl.when(has_next)
    def _():
        for d in range(panels):
            pl.semaphore_signal(barrier, inc=1, device_id={
                "panel": lax.rem(panel + d, panels), "slab": slab + 1}, device_id_type=MESH)

    @pl.when(has_prev)
    def _():
        for d in range(panels):
            pl.semaphore_signal(barrier, inc=1, device_id={
                "panel": lax.rem(panel + d, panels), "slab": slab - 1}, device_id_type=MESH)

    for copy in smalls[1:]:
        copy.wait()
    position = 3.0 + offset_ref[...].astype(jnp.float32) * 0.125
    terms = [position - float(m) for m in range(TAPS)]
    before = [None] * TAPS
    after = [None] * TAPS
    for k in range(1, TAPS):
        before[k] = terms[k - 1] if k == 1 else before[k - 1] * terms[k - 1]
    for k in range(TAPS - 2, -1, -1):
        after[k] = terms[k + 1] if k == TAPS - 2 else after[k + 1] * terms[k + 1]
    for k in range(TAPS):
        scale = 1.0 / math.prod(k - m for m in range(TAPS) if m != k)
        if k == 0:
            value = after[k]
        elif k == TAPS - 1:
            value = before[k]
        else:
            value = before[k] * after[k]
        weight_ref[k] = value * scale
    live = live_ref[panel]
    group_of = lax.broadcasted_iota(jnp.int32, (observers, blocks), 1) // GB
    delay_ref[...] = jnp.where(group_of < live, delay_ref[...], 4 * LAGS)

    smalls[0].wait()
    green_f32[...] = green_in[...].astype(jnp.float32)
    block_row = lax.broadcasted_iota(jnp.int32, (BP, KT), 0)
    panel_col = lax.broadcasted_iota(jnp.int32, (BP, KT), 1)
    diagonal = jnp.where(panel_col // BP == block_row, 1.0, 0.0).astype(jnp.bfloat16)

    def tile_step(tile, carry):
        columns = pl.ds(pl.multiple_of(tile * KT, KT), KT)
        pieces = []
        for o in range(observers):
            row = jnp.broadcast_to(green_f32[o:o + 1, columns], (BP, KT)).astype(jnp.bfloat16)
            pieces.append(row * diagonal)
        spread = jnp.concatenate(pieces, axis=0)
        product = jnp.dot(spread, load_ref[columns, :], preferred_element_type=jnp.float32)
        block_ref[:, pl.ds(pl.multiple_of(tile * BP, BP), BP), :] = (
            product.astype(jnp.bfloat16).reshape(observers, BP, samples))
        return carry

    tiles_per_load = tiles // LOAD_CHUNKS
    for c in range(LOAD_CHUNKS):
        loads[c].wait()
        lax.fori_loop(c * tiles_per_load, (c + 1) * tiles_per_load, tile_step, 0)

    sub = lax.broadcasted_iota(jnp.int32, (BP, blocks), 0)
    lane = lax.broadcasted_iota(jnp.int32, (8, LANES), 1)
    row8 = lax.broadcasted_iota(jnp.int32, (8, LANES), 0)
    wide = samples // LANES
    zero = jnp.zeros((8, LANES), jnp.float32)

    def shifted_in(parts, keep):
        return [jnp.where(keep, parts[0], 0.0)] + [
            jnp.where(keep, parts[j], parts[j - 1]) for j in range(1, len(parts))]

    def observer_step(o, carry):
        behind = sub - delay_ref[pl.ds(o, 1), :]
        tap = behind & (BP - 1)
        place = ((BP - 1 - behind) >> 4).astype(jnp.float32).astype(jnp.bfloat16)
        stencil = jnp.zeros((BP, blocks), jnp.float32)
        for k in range(TAPS):
            stencil = jnp.where(tap == k, weight_ref[k, pl.ds(o, 1), :], stencil)
        stencil = stencil.astype(jnp.bfloat16)
        table = jnp.concatenate([
            jnp.where(place == jnp.bfloat16(q), stencil, jnp.bfloat16(0)) for q in range(LAGS // BP)], axis=0)
        lagged = jnp.dot(table, block_ref[o], preferred_element_type=jnp.float32)
        sums = [zero] * (wide + 1)
        for high in range(LAGS // 8):
            shift = 8 * high
            parts = [lagged[shift:shift + 8, j * LANES:(j + 1) * LANES] for j in range(wide)]
            if shift == 0:
                moved = parts + [None]
            else:
                parts = [pltpu.roll(part, shift, 1) for part in parts]
                keep = lane >= shift
                moved = shifted_in(parts, keep) + [jnp.where(keep, 0.0, parts[-1])]
            sums = [a if b is None else a + b for a, b in zip(sums, moved)]
        sums = [pltpu.roll(part, 0, 1, stride=1, stride_axis=0) for part in sums]
        sums = shifted_in(sums, lane >= row8)
        own = row8 == lax.rem(o, ROWS)
        return tuple(
            jnp.where(own, jnp.sum(part, axis=0, keepdims=True), kept) for part, kept in zip(sums, carry))

    def main_copy(c, d):
        return pltpu.make_async_remote_copy(
            src_ref=part_ref.at[pl.ds(c * ROWS, ROWS), pl.ds(0, samples)],
            dst_ref=main_in.at[c, d - 1],
            send_sem=main_send.at[c, d - 1], recv_sem=main_recv.at[c, d - 1],
            device_id={"panel": lax.rem(panel + d, panels)}, device_id_type=MESH)

    def tail_copy(c, d):
        return pltpu.make_async_remote_copy(
            src_ref=part_ref.at[pl.ds(c * ROWS, ROWS), pl.ds(samples, LAGS)],
            dst_ref=tail_in.at[c, d],
            send_sem=tail_send.at[c, d], recv_sem=tail_recv.at[c, d],
            device_id={"panel": lax.rem(panel + d, panels), "slab": slab + 1}, device_id_type=MESH)

    for c in range(chunks):
        gathered = lax.fori_loop(
            c * ROWS, (c + 1) * ROWS, observer_step, (zero,) * (wide + 1), unroll=UNROLL)
        for j in range(wide + 1):
            part_ref[c * ROWS:(c + 1) * ROWS, j * LANES:(j + 1) * LANES] = gathered[j]
        if c == 0:
            pl.semaphore_wait(barrier, panels - 1 + panels * (has_next.astype(jnp.int32) + has_prev.astype(jnp.int32)))

        for d in range(1, panels):
            main_copy(c, d).start()

        @pl.when(has_next)
        def _():
            for d in range(panels):
                tail_copy(c, d).start()

    for c in range(chunks):
        rows = slice(c * ROWS, (c + 1) * ROWS)
        total = part_ref[rows, :samples]
        for d in range(1, panels):
            main_copy(c, d).wait_recv()
            total = total + main_in[c, d - 1]
        out_ref[rows, :] = total

        @pl.when(has_prev)
        def _():
            late = None
            for d in range(panels):
                tail_copy(c, d).wait_recv()
                late = tail_in[c, d] if late is None else late + tail_in[c, d]
            out_ref[rows, :LAGS] += late

    for c in range(chunks):
        for d in range(1, panels):
            main_copy(c, d).wait_send()

        @pl.when(has_next)
        def _():
            for d in range(panels):
                tail_copy(c, d).wait_send()


def shards(panels, slabs, loading, green, delays, offsets, live_groups):
    n_panels, samples = loading.shape
    observers = green.shape[0]
    blocks = delays.shape[1]
    chunks = observers // ROWS
    peers = max(panels - 1, 1)
    anywhere = pl.BlockSpec(memory_space=pl.ANY)
    return pl.pallas_call(
        functools.partial(kernel, panels, slabs),
        out_shape=jax.ShapeDtypeStruct((observers, samples), jnp.float32),
        in_specs=[pl.BlockSpec(memory_space=pltpu.SMEM)] + [anywhere] * 4,
        out_specs=pl.BlockSpec(memory_space=pltpu.VMEM),
        scratch_shapes=[
            pltpu.VMEM((n_panels, samples), jnp.bfloat16),
            pltpu.VMEM((observers, n_panels), jnp.bfloat16),
            pltpu.VMEM((observers, n_panels), jnp.float32),
            pltpu.VMEM((observers, blocks), jnp.int32),
            pltpu.VMEM((observers, blocks), jnp.int32),
            pltpu.VMEM((TAPS, observers, blocks), jnp.float32),
            pltpu.VMEM((observers, blocks, samples), jnp.bfloat16),
            pltpu.VMEM((observers, samples + LAGS), jnp.float32),
            pltpu.VMEM((chunks, peers, ROWS, samples), jnp.float32),
            pltpu.VMEM((chunks, panels, ROWS, LAGS), jnp.float32),
            pltpu.SemaphoreType.DMA((LOAD_CHUNKS,)),
            pltpu.SemaphoreType.DMA((3,)),
            pltpu.SemaphoreType.DMA((chunks, peers)),
            pltpu.SemaphoreType.DMA((chunks, peers)),
            pltpu.SemaphoreType.DMA((chunks, panels)),
            pltpu.SemaphoreType.DMA((chunks, panels)),
        ],
        compiler_params=pltpu.CompilerParams(
            collective_id=0, has_side_effects=True, vmem_limit_bytes=56 * 2 ** 20),
        name="far_field",
    )(live_groups, loading, green, delays, offsets)


def solution(mesh):
    placed = (
        P(("case", "panel"), "slab"),
        P(("case", "obs"), "panel"),
        P(("case", "obs"), "panel"),
        P(("case", "obs"), "panel"),
        P("case"),
    )
    return jax.shard_map(
        functools.partial(shards, mesh.shape["panel"], mesh.shape["slab"]),
        mesh=mesh, in_specs=placed, out_specs=P(("case", "obs"), "slab"), check_vma=False,
    )
```

time: 134 us -> 27 us (0.20)
  the two profiles are of different devices: /device:TPU:6 before, /device:TPU:0 now
where the time goes in v1:
time: 27 us; the launch traced here: 26.8 us
  Pallas kernels  25.4 us (94%)
  local copies, waits for them, and re-layouts  1.38 us (5%)
    pallas_call x1, Pallas kernels, shards(): pl.pallas_call(functools.partial(kernel, panels, slabs), out_shape=jax.Sh...  25.4 us
    unnamed x1, local copies, waits for them, and re-layouts  1.38 us

profile of v1, /device:TPU:0, one launch (start us, length us, event | category | flops | bytes accessed | tf_op | source)
XLA Modules:
  0.0 26.8 jit_solution(2481567620729734569)
XLA Ops:
  0.0 25.4 %far_field.1 = f32[32,256]{1,0:T(8,128)} custom-call(s32[4]{0:T(128)} %live_ref.1, bf16[8192,256]{1,0:T(8,128)(2,1)} %load_hbm.1, bf16[32,8192]{1,0:T(8,128)(2,1)} %green_hbm.1, s32[32,512]{1,0:T(8,128)} %delay_hbm.1, s32[32,512]{1,0:T(8,128)} %offset_hbm.1), custom_call_target="tpu_custom_call" | custom-call | tf_op jit(solution)/shard_map/far_field/pallas_call | solution.py:210
  25.4 1.4 %copy.7 = f32[32,256]{1,0:T(8,128)} copy(f32[32,256]{1,0:T(8,128)} %far_field.1) | data formatting | bytes 65536

commit v2 on v1

--- a/solution.py
+++ b/solution.py
@@ -16,13 +16,13 @@
 LANES = 128
 ROWS = 8
 LOAD_CHUNKS = 8
-UNROLL = 2
+UNROLL = 8
 MESH = pl.DeviceIdType.MESH
 
 
 def kernel(panels, slabs, live_ref, load_hbm, green_hbm, delay_hbm, offset_hbm, out_ref,
            load_ref, green_in, green_f32, delay_ref, offset_ref, weight_ref, block_ref, part_ref,
-           main_in, tail_in, load_sem, small_sem, main_send, main_recv, tail_send, tail_recv):
+           main_out, tail_out, main_in, tail_in, load_sem, green_sem, small_sem, main_send, main_recv, tail_send, tail_recv):
     panel = lax.axis_index("panel")
     slab = lax.axis_index("slab")
     n_panels, samples = load_hbm.shape
@@ -35,14 +35,16 @@
     has_prev = slab > 0
 
     smalls = [pltpu.make_async_copy(src, dst, small_sem.at[i]) for i, (src, dst) in enumerate(
-        ((green_hbm, green_in), (delay_hbm, delay_ref), (offset_hbm, offset_ref)))]
+        ((delay_hbm, delay_ref), (offset_hbm, offset_ref)))]
+    loads, greens = [], []
+    for c in range(LOAD_CHUNKS):
+        rows = pl.ds(c * per_load, per_load)
+        greens.append(pltpu.make_async_copy(green_hbm.at[:, rows], green_in.at[:, rows], green_sem.at[c]))
+        greens[-1].start()
+        loads.append(pltpu.make_async_copy(load_hbm.at[rows, :], load_ref.at[rows, :], load_sem.at[c]))
+        loads[-1].start()
     for copy in smalls:
         copy.start()
-    loads = []
-    for c in range(LOAD_CHUNKS):
-        rows = pl.ds(c * per_load, per_load)
-        loads.append(pltpu.make_async_copy(load_hbm.at[rows, :], load_ref.at[rows, :], load_sem.at[c]))
-        loads[-1].start()
 
     barrier = pltpu.get_barrier_semaphore()
     for d in range(1, panels):
@@ -60,7 +62,31 @@
             pl.semaphore_signal(barrier, inc=1, device_id={
                 "panel": lax.rem(panel + d, panels), "slab": slab - 1}, device_id_type=MESH)
 
-    for copy in smalls[1:]:
+    block_row = lax.broadcasted_iota(jnp.int32, (BP, KT), 0)
+    panel_col = lax.broadcasted_iota(jnp.int32, (BP, KT), 1)
+    diagonal = jnp.where(panel_col // BP == block_row, 1.0, 0.0).astype(jnp.bfloat16)
+
+    def tile_step(tile, carry):
+        columns = pl.ds(pl.multiple_of(tile * KT, KT), KT)
+        pieces = []
+        for o in range(observers):
+            row = jnp.broadcast_to(green_f32[o:o + 1, columns], (BP, KT)).astype(jnp.bfloat16)
+            pieces.append(row * diagonal)
+        spread = jnp.concatenate(pieces, axis=0)
+        product = jnp.dot(spread, load_ref[columns, :], preferred_element_type=jnp.float32)
+        block_ref[:, pl.ds(pl.multiple_of(tile * BP, BP), BP), :] = (
+            product.astype(jnp.bfloat16).reshape(observers, BP, samples))
+        return carry
+
+    tiles_per_load = tiles // LOAD_CHUNKS
+    for c in range(LOAD_CHUNKS):
+        greens[c].wait()
+        columns = slice(c * per_load, (c + 1) * per_load)
+        green_f32[:, columns] = green_in[:, columns].astype(jnp.float32)
+        loads[c].wait()
+        lax.fori_loop(c * tiles_per_load, (c + 1) * tiles_per_load, tile_step, 0, unroll=4)
+
+    for copy in smalls:
         copy.wait()
     position = 3.0 + offset_ref[...].astype(jnp.float32) * 0.125
     terms = [position - float(m) for m in range(TAPS)]
@@ -82,29 +108,6 @@
     live = live_ref[panel]
     group_of = lax.broadcasted_iota(jnp.int32, (observers, blocks), 1) // GB
     delay_ref[...] = jnp.where(group_of < live, delay_ref[...], 4 * LAGS)
-
-    smalls[0].wait()
-    green_f32[...] = green_in[...].astype(jnp.float32)
-    block_row = lax.broadcasted_iota(jnp.int32, (BP, KT), 0)
-    panel_col = lax.broadcasted_iota(jnp.int32, (BP, KT), 1)
-    diagonal = jnp.where(panel_col // BP == block_row, 1.0, 0.0).astype(jnp.bfloat16)
-
-    def tile_step(tile, carry):
-        columns = pl.ds(pl.multiple_of(tile * KT, KT), KT)
-        pieces = []
-        for o in range(observers):
-            row = jnp.broadcast_to(green_f32[o:o + 1, columns], (BP, KT)).astype(jnp.bfloat16)
-            pieces.append(row * diagonal)
-        spread = jnp.concatenate(pieces, axis=0)
-        product = jnp.dot(spread, load_ref[columns, :], preferred_element_type=jnp.float32)
-        block_ref[:, pl.ds(pl.multiple_of(tile * BP, BP), BP), :] = (
-            product.astype(jnp.bfloat16).reshape(observers, BP, samples))
-        return carry
-
-    tiles_per_load = tiles // LOAD_CHUNKS
-    for c in range(LOAD_CHUNKS):
-        loads[c].wait()
-        lax.fori_loop(c * tiles_per_load, (c + 1) * tiles_per_load, tile_step, 0)
 
     sub = lax.broadcasted_iota(jnp.int32, (BP, blocks), 0)
     lane = lax.broadcasted_iota(jnp.int32, (8, LANES), 1)
@@ -146,14 +149,14 @@
 
     def main_copy(c, d):
         return pltpu.make_async_remote_copy(
-            src_ref=part_ref.at[pl.ds(c * ROWS, ROWS), pl.ds(0, samples)],
+            src_ref=main_out.at[c],
             dst_ref=main_in.at[c, d - 1],
             send_sem=main_send.at[c, d - 1], recv_sem=main_recv.at[c, d - 1],
             device_id={"panel": lax.rem(panel + d, panels)}, device_id_type=MESH)
 
     def tail_copy(c, d):
         return pltpu.make_async_remote_copy(
-            src_ref=part_ref.at[pl.ds(c * ROWS, ROWS), pl.ds(samples, LAGS)],
+            src_ref=tail_out.at[c],
             dst_ref=tail_in.at[c, d],
             send_sem=tail_send.at[c, d], recv_sem=tail_recv.at[c, d],
             device_id={"panel": lax.rem(panel + d, panels), "slab": slab + 1}, device_id_type=MESH)
@@ -161,8 +164,11 @@
     for c in range(chunks):
         gathered = lax.fori_loop(
             c * ROWS, (c + 1) * ROWS, observer_step, (zero,) * (wide + 1), unroll=UNROLL)
-        for j in range(wide + 1):
-            part_ref[c * ROWS:(c + 1) * ROWS, j * LANES:(j + 1) * LANES] = gathered[j]
+        for j in range(wide):
+            lanes = slice(j * LANES, (j + 1) * LANES)
+            part_ref[c * ROWS:(c + 1) * ROWS, lanes] = gathered[j]
+            main_out[c, :, lanes] = gathered[j].astype(jnp.bfloat16)
+        tail_out[c] = gathered[wide].astype(jnp.bfloat16)
         if c == 0:
             pl.semaphore_wait(barrier, panels - 1 + panels * (has_next.astype(jnp.int32) + has_prev.astype(jnp.int32)))
 
@@ -176,10 +182,10 @@
 
     for c in range(chunks):
         rows = slice(c * ROWS, (c + 1) * ROWS)
-        total = part_ref[rows, :samples]
+        total = part_ref[rows, :]
         for d in range(1, panels):
             main_copy(c, d).wait_recv()
-            total = total + main_in[c, d - 1]
+            total = total + main_in[c, d - 1].astype(jnp.float32)
         out_ref[rows, :] = total
 
         @pl.when(has_prev)
@@ -187,7 +193,8 @@
             late = None
             for d in range(panels):
                 tail_copy(c, d).wait_recv()
-                late = tail_in[c, d] if late is None else late + tail_in[c, d]
+                term = tail_in[c, d].astype(jnp.float32)
+                late = term if late is None else late + term
             out_ref[rows, :LAGS] += late
 
     for c in range(chunks):
@@ -220,11 +227,14 @@
             pltpu.VMEM((observers, blocks), jnp.int32),
             pltpu.VMEM((TAPS, observers, blocks), jnp.float32),
             pltpu.VMEM((observers, blocks, samples), jnp.bfloat16),
-            pltpu.VMEM((observers, samples + LAGS), jnp.float32),
-            pltpu.VMEM((chunks, peers, ROWS, samples), jnp.float32),
-            pltpu.VMEM((chunks, panels, ROWS, LAGS), jnp.float32),
+            pltpu.VMEM((observers, samples), jnp.float32),
+            pltpu.VMEM((chunks, ROWS, samples), jnp.bfloat16),
+            pltpu.VMEM((chunks, ROWS, LAGS), jnp.bfloat16),
+            pltpu.VMEM((chunks, peers, ROWS, samples), jnp.bfloat16),
+            pltpu.VMEM((chunks, panels, ROWS, LAGS), jnp.bfloat16),
             pltpu.SemaphoreType.DMA((LOAD_CHUNKS,)),
-            pltpu.SemaphoreType.DMA((3,)),
+            pltpu.SemaphoreType.DMA((LOAD_CHUNKS,)),
+            pltpu.SemaphoreType.DMA((2,)),
             pltpu.SemaphoreType.DMA((chunks, peers)),
             pltpu.SemaphoreType.DMA((chunks, peers)),
             pltpu.SemaphoreType.DMA((chunks, panels)),

time: 27 us -> 18 us (0.67)
  Pallas kernels: 25.4 us -> 16.4 us
    pallas_call x1, Pallas kernels: 25.4 us -> 16.4 us  [shards(): pl.pallas_call(functools.partial(kernel, panels, slabs), out_shape=jax.Sh...]
where the time goes in v2:
time: 18 us; the launch traced here: 17.8 us
  Pallas kernels  16.4 us (91%)
  local copies, waits for them, and re-layouts  1.38 us (8%)
    pallas_call x1, Pallas kernels, shards(): pl.pallas_call(functools.partial(kernel, panels, slabs), out_shape=jax.Sh...  16.4 us
    unnamed x1, local copies, waits for them, and re-layouts  1.38 us

profile of v2, /device:TPU:0, one launch (start us, length us, event | category | flops | bytes accessed | tf_op | source)
XLA Modules:
  0.0 17.8 jit_solution(15305858079915881805)
XLA Ops:
  0.0 16.4 %far_field.1 = f32[32,256]{1,0:T(8,128)} custom-call(s32[4]{0:T(128)} %live_ref.1, bf16[8192,256]{1,0:T(8,128)(2,1)} %load_hbm.1, bf16[32,8192]{1,0:T(8,128)(2,1)} %green_hbm.1, s32[32,512]{1,0:T(8,128)} %delay_hbm.1, s32[32,512]{1,0:T(8,128)} %offset_hbm.1), custom_call_target="tpu_custom_call" | custom-call | tf_op jit(solution)/shard_map/far_field/pallas_call | solution.py:217
  16.4 1.4 %copy.7 = f32[32,256]{1,0:T(8,128)} copy(f32[32,256]{1,0:T(8,128)} %far_field.1) | data formatting | bytes 65536

commit v3 on v2

--- a/solution.py
+++ b/solution.py
@@ -15,13 +15,14 @@
 KT = 256
 LANES = 128
 ROWS = 8
-LOAD_CHUNKS = 8
+SHARES = (2, 6, 8, 16)
 UNROLL = 8
+TILE_UNROLL = 4
 MESH = pl.DeviceIdType.MESH
 
 
-def kernel(panels, slabs, live_ref, load_hbm, green_hbm, delay_hbm, offset_hbm, out_ref,
-           load_ref, green_in, green_f32, delay_ref, offset_ref, weight_ref, block_ref, part_ref,
+def kernel(panels, slabs, live_hbm, load_hbm, green_hbm, delay_hbm, offset_hbm, out_ref,
+           live_ref, load_ref, green_in, green_f32, delay_ref, offset_ref, weight_ref, block_ref, part_ref,
            main_out, tail_out, main_in, tail_in, load_sem, green_sem, small_sem, main_send, main_recv, tail_send, tail_recv):
     panel = lax.axis_index("panel")
     slab = lax.axis_index("slab")
@@ -30,15 +31,15 @@
     blocks = delay_hbm.shape[1]
     chunks = observers // ROWS
     tiles = n_panels // KT
-    per_load = n_panels // LOAD_CHUNKS
+    edges = [tiles * sum(SHARES[:c]) // sum(SHARES) for c in range(len(SHARES) + 1)]
     has_next = slab < slabs - 1
     has_prev = slab > 0
 
     smalls = [pltpu.make_async_copy(src, dst, small_sem.at[i]) for i, (src, dst) in enumerate(
-        ((delay_hbm, delay_ref), (offset_hbm, offset_ref)))]
+        ((delay_hbm, delay_ref), (offset_hbm, offset_ref), (live_hbm, live_ref)))]
     loads, greens = [], []
-    for c in range(LOAD_CHUNKS):
-        rows = pl.ds(c * per_load, per_load)
+    for c in range(len(SHARES)):
+        rows = pl.ds(edges[c] * KT, (edges[c + 1] - edges[c]) * KT)
         greens.append(pltpu.make_async_copy(green_hbm.at[:, rows], green_in.at[:, rows], green_sem.at[c]))
         greens[-1].start()
         loads.append(pltpu.make_async_copy(load_hbm.at[rows, :], load_ref.at[rows, :], load_sem.at[c]))
@@ -78,13 +79,12 @@
             product.astype(jnp.bfloat16).reshape(observers, BP, samples))
         return carry
 
-    tiles_per_load = tiles // LOAD_CHUNKS
-    for c in range(LOAD_CHUNKS):
+    for c in range(len(SHARES)):
         greens[c].wait()
-        columns = slice(c * per_load, (c + 1) * per_load)
+        columns = slice(edges[c] * KT, edges[c + 1] * KT)
         green_f32[:, columns] = green_in[:, columns].astype(jnp.float32)
         loads[c].wait()
-        lax.fori_loop(c * tiles_per_load, (c + 1) * tiles_per_load, tile_step, 0, unroll=4)
+        lax.fori_loop(edges[c], edges[c + 1], tile_step, 0, unroll=True)
 
     for copy in smalls:
         copy.wait()
@@ -213,13 +213,14 @@
     blocks = delays.shape[1]
     chunks = observers // ROWS
     peers = max(panels - 1, 1)
-    anywhere = pl.BlockSpec(memory_space=pl.ANY)
+    anywhere = pl.BlockSpec(memory_space=pltpu.HBM)
     return pl.pallas_call(
         functools.partial(kernel, panels, slabs),
         out_shape=jax.ShapeDtypeStruct((observers, samples), jnp.float32),
-        in_specs=[pl.BlockSpec(memory_space=pltpu.SMEM)] + [anywhere] * 4,
+        in_specs=[anywhere] * 5,
         out_specs=pl.BlockSpec(memory_space=pltpu.VMEM),
         scratch_shapes=[
+            pltpu.SMEM((panels,), jnp.int32),
             pltpu.VMEM((n_panels, samples), jnp.bfloat16),
             pltpu.VMEM((observers, n_panels), jnp.bfloat16),
             pltpu.VMEM((observers, n_panels), jnp.float32),
@@ -232,18 +233,18 @@
             pltpu.VMEM((chunks, ROWS, LAGS), jnp.bfloat16),
             pltpu.VMEM((chunks, peers, ROWS, samples), jnp.bfloat16),
             pltpu.VMEM((chunks, panels, ROWS, LAGS), jnp.bfloat16),
-            pltpu.SemaphoreType.DMA((LOAD_CHUNKS,)),
-            pltpu.SemaphoreType.DMA((LOAD_CHUNKS,)),
-            pltpu.SemaphoreType.DMA((2,)),
+            pltpu.SemaphoreType.DMA((len(SHARES),)),
+            pltpu.SemaphoreType.DMA((len(SHARES),)),
+            pltpu.SemaphoreType.DMA((3,)),
             pltpu.SemaphoreType.DMA((chunks, peers)),
             pltpu.SemaphoreType.DMA((chunks, peers)),
             pltpu.SemaphoreType.DMA((chunks, panels)),
             pltpu.SemaphoreType.DMA((chunks, panels)),
         ],
         compiler_params=pltpu.CompilerParams(
-            collective_id=0, has_side_effects=True, vmem_limit_bytes=56 * 2 ** 20),
+            collective_id=0, has_side_effects=True, vmem_limit_bytes=24 * 2 ** 20),
         name="far_field",
-    )(live_groups, loading, green, delays, offsets)
+    )(*(pltpu.with_memory_space_constraint(x, pltpu.HBM) for x in (live_groups, loading, green, delays, offsets)))
 
 
 def solution(mesh):

time: 18 us -> 15.1 us (0.84)
  Pallas kernels: 16.4 us -> 14.3 us
  local copies, waits for them, and re-layouts: 1.38 us -> 0.62 us
    pallas_call x1, Pallas kernels: 16.4 us -> 14.3 us  [shards(): pl.pallas_call(functools.partial(kernel, panels, slabs), out_shape=jax.Sh...]
    unnamed x1, local copies, waits for them, and re-layouts: 1.38 us -> 0.62 us
where the time goes in v3:
time: 15.1 us; the launch traced here: 14.9 us
  Pallas kernels  14.3 us (95%)
  local copies, waits for them, and re-layouts  0.62 us (4%)
    pallas_call x1, Pallas kernels, shards(): pl.pallas_call(functools.partial(kernel, panels, slabs), out_shape=jax.Sh...  14.3 us
    unnamed x1, local copies, waits for them, and re-layouts  0.62 us

profile of v3, /device:TPU:0, one launch (start us, length us, event | category | flops | bytes accessed | tf_op | source)
XLA Modules:
  0.0 14.9 jit_solution(10718165396338895818)
XLA Ops:
  0.0 14.3 %far_field.1 = f32[32,256]{1,0:T(8,128)S(1)} custom-call(s32[4]{0:T(128)} %live_hbm.1, bf16[8192,256]{1,0:T(8,128)(2,1)} %load_hbm.1, bf16[32,8192]{1,0:T(8,128)(2,1)} %green_hbm.1, s32[32,512]{1,0:T(8,128)} %delay_hbm.1, s32[32,512]{1,0:T(8,128)} %offset_hbm.1), custom_call_target="tpu_custom_call" | custom-call | tf_op jit(solution)/shard_map/far_field/pallas_call | solution.py:217
  14.3 0.6 %copy.7 = f32[32,256]{1,0:T(8,128)} copy(f32[32,256]{1,0:T(8,128)S(1)} %far_field.1) | data formatting | bytes 65536

commit v4 on v3

--- a/solution.py
+++ b/solution.py
@@ -17,12 +17,11 @@
 ROWS = 8
 SHARES = (2, 6, 8, 16)
 UNROLL = 8
-TILE_UNROLL = 4
 MESH = pl.DeviceIdType.MESH
 
 
 def kernel(panels, slabs, live_hbm, load_hbm, green_hbm, delay_hbm, offset_hbm, out_ref,
-           live_ref, load_ref, green_in, green_f32, delay_ref, offset_ref, weight_ref, block_ref, part_ref,
+           live_ref, load_ref, green_in, delay_ref, offset_ref, weight_ref, block_ref, part_ref,
            main_out, tail_out, main_in, tail_in, load_sem, green_sem, small_sem, main_send, main_recv, tail_send, tail_recv):
     panel = lax.axis_index("panel")
     slab = lax.axis_index("slab")
@@ -71,7 +70,7 @@
         columns = pl.ds(pl.multiple_of(tile * KT, KT), KT)
         pieces = []
         for o in range(observers):
-            row = jnp.broadcast_to(green_f32[o:o + 1, columns], (BP, KT)).astype(jnp.bfloat16)
+            row = jnp.broadcast_to(green_in[o:o + 1, columns], (BP, KT))
             pieces.append(row * diagonal)
         spread = jnp.concatenate(pieces, axis=0)
         product = jnp.dot(spread, load_ref[columns, :], preferred_element_type=jnp.float32)
@@ -81,8 +80,6 @@
 
     for c in range(len(SHARES)):
         greens[c].wait()
-        columns = slice(edges[c] * KT, edges[c + 1] * KT)
-        green_f32[:, columns] = green_in[:, columns].astype(jnp.float32)
         loads[c].wait()
         lax.fori_loop(edges[c], edges[c + 1], tile_step, 0, unroll=True)
 
@@ -223,7 +220,6 @@
             pltpu.SMEM((panels,), jnp.int32),
             pltpu.VMEM((n_panels, samples), jnp.bfloat16),
             pltpu.VMEM((observers, n_panels), jnp.bfloat16),
-            pltpu.VMEM((observers, n_panels), jnp.float32),
             pltpu.VMEM((observers, blocks), jnp.int32),
             pltpu.VMEM((observers, blocks), jnp.int32),
             pltpu.VMEM((TAPS, observers, blocks), jnp.float32),

time: 15.1 us -> 15 us (level)
  no operation moved by 1% of the time
where the time goes in v4:
time: 15 us; the launch traced here: 14.9 us
  Pallas kernels  14.3 us (95%)
  local copies, waits for them, and re-layouts  0.62 us (4%)
    pallas_call x1, Pallas kernels, shards(): pl.pallas_call(functools.partial(kernel, panels, slabs), out_shape=jax.Sh...  14.3 us
    unnamed x1, local copies, waits for them, and re-layouts  0.62 us

profile of v4, /device:TPU:0, one launch (start us, length us, event | category | flops | bytes accessed | tf_op | source)
XLA Modules:
  0.0 14.9 jit_solution(13283158036729754667)
XLA Ops:
  0.0 14.3 %far_field.1 = f32[32,256]{1,0:T(8,128)S(1)} custom-call(s32[4]{0:T(128)} %live_hbm.1, bf16[8192,256]{1,0:T(8,128)(2,1)} %load_hbm.1, bf16[32,8192]{1,0:T(8,128)(2,1)} %green_hbm.1, s32[32,512]{1,0:T(8,128)} %delay_hbm.1, s32[32,512]{1,0:T(8,128)} %offset_hbm.1), custom_call_target="tpu_custom_call" | custom-call | tf_op jit(solution)/shard_map/far_field/pallas_call | solution.py:214
  14.3 0.6 %copy.7 = f32[32,256]{1,0:T(8,128)} copy(f32[32,256]{1,0:T(8,128)S(1)} %far_field.1) | data formatting | bytes 65536
